TPU v7x, 32 devices: a whole 2x2x4 slice. The times are simulated.
32 devices in a mesh: region: 4 (over x, core), tile: 8 (over z, y).
Axes of the slice: x: 2, y: 2, z: 4, core: 2. Of those that a mesh axis runs over, the one named last changes fastest.
Arguments:
- quantized: bfloat16 [131072, 1024], P(('region', 'tile')), may hold values from -6 to 6
- block_scales: float32 [8, 131072], P(None, ('region', 'tile')), may hold values from 0.25 to 4
- band_width: int32 [32], replicated, may hold values from 1 to 256, as said below
- valid_count: int32 [32], P(('region', 'tile')), may hold values from 1024 to 4096, as said below
- prior_basis: float32 [1024, 64], replicated, may hold values from -0.1875 to 0.1875
Outputs:
- projected: float32 [64, 131072], P(None, ('region', 'tile'))
- new_basis: float32 [1024, 64], replicated
Inputs may be any that keep to these rules, and one draw needn't show every extreme that they name: `band_width`: some tile other than the first of its region has width 256 in every draw. `valid_count`: the last tile's count is 4096 in every draw.
All inputs are finite; a program needn't handle non-finite values.
Results may differ from a plain program's by a relative error of at most 0.0016.
Values may be sent and summed in bfloat16 or wider, within the bound.
A program may use at most 128 MiB of HBM per device.

v0:
```python
import jax
import jax.numpy as jnp
from jax import lax
from jax.sharding import PartitionSpec as P

BAND = 256


def padded_2(cells, sides, width):
    for axis, dim in sides:
        count = lax.axis_size(axis)
        ends = count - 1
        head = lax.slice_in_dim(cells, 0, width, axis=dim)
        tail = lax.slice_in_dim(cells, cells.shape[dim] - width, cells.shape[dim], axis=dim)
        cells = jnp.concatenate(
            [
                lax.ppermute(tail, axis, [(i, (i + 1) % count) for i in range(ends)]),
                cells,
                lax.ppermute(head, axis, [((i + 1) % count, i) for i in range(ends)]),
            ],
            axis=dim,
        )
    return cells


def dequantize(quantized, block_scales):
    tok_rows, feat_dim = quantized.shape
    groups = block_scales.shape[0]
    blocks = (
        quantized.astype(jnp.float32).reshape(tok_rows, groups, feat_dim // groups)
        * block_scales.T[:, :, None]
    )
    return blocks.reshape(tok_rows, feat_dim).astype(jnp.bfloat16)


def blend(initial, neighbour, chosen):
    summed = (initial.astype(jnp.float32) + neighbour.astype(jnp.float32)) * 0.5
    return jnp.where(chosen[:, None], summed, initial.astype(jnp.float32)).astype(jnp.bfloat16)


def finish(update, cross_sum, centred, spread):
    factor = jnp.linalg.cholesky(cross_sum)
    own_basis = jax.scipy.linalg.solve_triangular(factor, update.T, lower=True).T
    new_basis = spread(own_basis)
    projected = lax.dot_general(
        new_basis, centred, (((0,), (1,)), ((), ())), precision=lax.Precision.HIGHEST
    )
    return (projected, new_basis)


def per_device(quantized, block_scales, band_width, valid_count, prior_basis):
    tok_rows, feat_dim = quantized.shape
    n_region = lax.axis_size("region")
    n_tile = lax.axis_size("tile")
    devices = n_region * n_tile
    region_index = lax.axis_index("region")
    tile_index = lax.axis_index("tile")
    tile_number = region_index * n_tile + tile_index
    restored = dequantize(quantized, block_scales)
    padded = padded_2(restored, (("tile", 0),), BAND)
    prev_tail = padded[:BAND]
    next_head = padded[tok_rows + BAND :]
    left_width = jnp.where(tile_index > 0, band_width[tile_number], 0)
    right_width = jnp.where(
        tile_index < n_tile - 1, band_width[jnp.minimum(tile_number + 1, devices - 1)], 0
    )
    positions = jnp.arange(BAND)
    blank = jnp.zeros((BAND, feat_dim), jnp.bfloat16)
    left_part = lax.dynamic_slice_in_dim(
        jnp.concatenate([prev_tail, blank], 0), BAND - left_width, BAND, 0
    )
    right_part = lax.dynamic_slice_in_dim(
        jnp.concatenate([blank, next_head], 0), right_width, BAND, 0
    )
    new_head = blend(restored[:BAND], left_part, positions < left_width)
    new_tail = blend(restored[tok_rows - BAND :], right_part, positions >= BAND - right_width)
    blended = jnp.concatenate([new_head, restored[BAND : tok_rows - BAND], new_tail], 0)
    usable = jnp.arange(tok_rows) < valid_count[0]
    masked = jnp.where(usable[:, None], blended, jnp.zeros((), jnp.bfloat16))
    indicator = jnp.ones((tok_rows,), jnp.bfloat16)
    local_sums = jnp.dot(indicator, masked, preferred_element_type=jnp.float32)
    local_count = valid_count[0].astype(jnp.float32)
    masked_wide = masked.astype(jnp.float32)
    reduced = jnp.dot(masked_wide, prior_basis, precision=lax.Precision.HIGHEST)
    local_update = lax.dot_general(
        masked_wide, reduced, (((0,), (0,)), ((), ())), precision=lax.Precision.HIGHEST
    )
    summed_update, feature_sums, token_count = lax.psum(
        (local_update, local_sums, local_count), ("region", "tile")
    )
    average = feature_sums / token_count
    mean_image = jnp.dot(average, prior_basis, precision=lax.Precision.HIGHEST)
    update = summed_update - jnp.outer(feature_sums, mean_image)
    centred = jnp.where(usable[:, None], masked_wide - average, 0.0)
    cross_sum = jnp.dot(update.T, update, precision=lax.Precision.HIGHEST)
    return finish(update, cross_sum, centred, lambda block: block)


def solution(mesh):
    return jax.shard_map(
        per_device,
        mesh=mesh,
        in_specs=(
            P(("region", "tile"), None),
            P(None, ("region", "tile")),
            P(),
            P(("region", "tile")),
            P(),
        ),
        out_specs=(P(None, ("region", "tile")), P()),
        check_vma=False,
    )
```

profile of v0, /device:TPU:0, one launch (start us, length us, event | category | flops | bytes accessed | tf_op | source)
XLA Modules:
  0.0 243.6 jit_solution(15910361438467005526)
XLA Ops:
  7.2 0.0 copy-start
  7.2 0.0 all-reduce.5.cloned.1.call-start
  7.2 1.5 copy.7
  8.8 4.6 %mul.34 = f32[4096,8,128]{2,1,0:T(8,128)S(1)} broadcast(f32[4096,8]{1,0:T(8,128)S(1)} %copy.7), dimensions={0,1} | broadcast | bytes 16908288 | tf_op jit(solution)/shard_map/mul | solution.py:30
  13.4 7.7 %fusion = bf16[4096,1024]{1,0:T(8,128)(2,1)S(1)} fusion(f32[512,8,8,128]{3,2,1,0:T(8,128)S(1)} %bitcast.33, bf16[4096,1024]{1,0:T(8,128)(2,1)} %param.5), kind=kLoop, calls=%fused_computation.1 | loop fusion | flops 12582912 | bytes 33554432 | tf_op jit(solution)/shard_map/convert_element_type | solution.py:33
  21.1 3.2 %copy-done.2 = bf16[4096,1024]{1,0:T(8,128)(2,1)} copy-done((bf16[4096,1024]{1,0:T(8,128)(2,1)}, bf16[4096,1024]{1,0:T(8,128)(2,1)S(1)}, u32[]{:S(2)}) %copy-start.2) | copy-done | bytes 8388632
  24.3 0.1 fusion.25
  24.4 4.9 %collective-permute-start = (bf16[256,1024]{1,0:T(8,128)(2,1)S(1)}, bf16[256,1024]{1,0:T(8,128)(2,1)S(1)}, u32[]{:S(2)}, u32[]{:S(2)}) collective-permute-start(bf16[256,1024]{1,0:T(8,128)(2,1)S(1)} %get-tuple-element.6), channel_id=1, source_target_pairs={{0,1},{1,2},{2,3},{3,4},{4,5},{5,6},{6,7},{8,9},{9,10},{10,11},{11... | collective-permute-start | bytes 1572872 | tf_op jit(solution)/shard_map/ppermute | solution.py:17
  29.3 1.3 collective-permute-start.1
  30.7 6.9 %slice.28 = bf16[3584,1024]{1,0:T(8,128)(2,1)} slice(bf16[4096,1024]{1,0:T(8,128)(2,1)} %copy-done.2), slice={[256:3840], [0:1024]} | slice | bytes 14680064 | tf_op jit(solution)/shard_map/slice | solution.py:77
  37.6 0.6 fusion.26
  40.2 11.5 %collective-permute-done = bf16[256,1024]{1,0:T(8,128)(2,1)S(1)} collective-permute-done((bf16[256,1024]{1,0:T(8,128)(2,1)S(1)}, bf16[256,1024]{1,0:T(8,128)(2,1)S(1)}, u32[]{:S(2)}, u32[]{:S(2)}) %collective-permute-start) | collective-permute-done | bytes 524320 | tf_op jit(solution)/shard_map/ppermute | solution.py:17
  51.7 0.0 collective-permute-done.1
  51.7 1.8 fusion.9
  53.6 6.2 %maximum_select_fusion = bf16[4096,1024]{1,0:T(8,128)(2,1)S(1)} fusion(bf16[256,1024]{1,0:T(8,128)(2,1)S(1)} %get-tuple-element.5, bf16[3584,1024]{1,0:T(8,128)(2,1)} %slice.28, bf16[256,1024]{1,0:T(8,128)(2,1)S(1)} %get-tuple-element.4, pred[4096]{0:T(1024)(128)(4,1)S(1)} %iota_compare_fusion.2), kind=kLoop, calls=%fused_computation.6 | loop fusion | flops 29360128 | bytes 16781312 | tf_op jit(solution)/shard_map/jit(_where)/select_n | solution.py:79
  59.8 1.2 fusion.21
  61.0 6.7 %fusion.27 = f32[4096,64]{1,0:T(8,128)S(1)} fusion(bf16[4096,1024]{1,0:T(8,128)(2,1)S(1)} %maximum_select_fusion, f32[1024,64]{0,1:T(8,128)S(1)} %copy-done), kind=kOutput, calls=%fused_computation.47 | convolution fusion | flops 3221225472 | bytes 9699328 | tf_op jit(solution)/shard_map/dot_general | solution.py:84
  67.7 5.3 %fusion.28 = f32[1024,64]{0,1:T(8,128)} fusion(bf16[4096,1024]{1,0:T(8,128)(2,1)S(1)} %maximum_select_fusion, f32[4096,64]{1,0:T(8,128)S(1)} %fusion.27), kind=kOutput, calls=%fused_computation.48 | convolution fusion | flops 3221225472 | bytes 9699328 | tf_op jit(solution)/shard_map/dot_general | solution.py:85
  73.0 0.0 all-reduce.5.cloned.1.call-update
  73.0 41.8 %all-reduce.2 = (f32[1024]{0:T(1024)S(1)}, f32[]{:T(128)}) all-reduce(f32[1024]{0:T(1024)S(1)} %bitcast.37, f32[]{:T(128)S(6)} %convert_element_type.40), channel_id=1, replica_groups=mesh['region'=4,'tile'=8] {'region','tile'}, use_global_device_ids=true, to_apply=%region_1.2 | all-reduce | flops 1025 | bytes 8200 | tf_op jit(solution)/shard_map/psum | solution.py:88
  114.7 0.6 broadcast_divide_fusion
  115.4 0.3 convolution_bitcast_fusion
  115.7 86.2 %all-reduce.5.cloned.1.call-done = f32[1024,64]{0,1:T(8,128)} async-done(((f32[1024,64]{0,1:T(8,128)}), f32[1024,64]{0,1:T(8,128)}) %all-reduce.5.cloned.1.call-update) | async-done | bytes 262160 | tf_op jit(solution)/shard_map/psum | solution.py:88
  201.9 1.5 fusion.13
  203.3 0.1 copy.8
  203.4 5.8 %cholesky.16 = f32[64,64]{1,0:T(8,128)S(1)} custom-call(f32[64,64]{1,0:T(8,128)S(1)} %fusion.20), custom_call_target="Cholesky" | custom-call | tf_op jit(solution)/shard_map/jit(cholesky)/cholesky | solution.py:42
  209.3 0.6 compare_reduce_fusion
  210.0 0.7 fusion.18
  210.6 4.9 %custom-call.7 = f32[1,64,64]{1,2,0:T(8,128)S(1)} custom-call(f32[1,64,64]{2,1,0:T(8,128)S(1)} %fusion.18), custom_call_target="InvertDiagBlocksLowerTriangular" | custom-call | tf_op jit(solution)/shard_map/jit(_solve_triangular)/triangular_solve | solution.py:43
  215.5 1.4 fusion.12
  216.9 0.0 copy-start.3
  217.0 19.8 %fusion.1 = f32[64,4096]{1,0:T(8,128)} fusion(f32[64,1024]{1,0:T(8,128)S(1)} %fusion.12, bf16[4096,1024]{1,0:T(8,128)(2,1)} %copy-done.1, f32[1024]{0:T(1024)S(1)} %broadcast_divide_fusion, pred[4096]{0:T(1024)(128)(4,1)S(1)} %iota_compare_fusion.2), kind=kOutput, calls=%fused_computation.2 | convolution fusion | flops 3233808384 | bytes 9707520 | tf_op jit(solution)/shard_map/dot_general | solution.py:45
  (11 shorter events, 0.1 us)
Async XLA Ops:
  7.2 53.9 %copy-start = (f32[1024,64]{0,1:T(8,128)S(1)}, f32[1024,64]{0,1:T(8,128)}, u32[]{:S(2)}) copy-start(f32[1024,64]{0,1:T(8,128)} %param.9) | copy-start | bytes 786436
  7.2 194.7 %all-reduce.5.cloned.1.call-start = ((), (), s32[]{:S(2)}) async-start(), calls=%async_computation | async-start | bytes 524288 | tf_op jit(solution)/shard_map/psum | solution.py:88
  21.1 3.2 %copy-start.2 = (bf16[4096,1024]{1,0:T(8,128)(2,1)}, bf16[4096,1024]{1,0:T(8,128)(2,1)S(1)}, u32[]{:S(2)}) copy-start(bf16[4096,1024]{1,0:T(8,128)(2,1)S(1)} %fusion) | copy-start | bytes 25165828
  24.3 13.3 %copy-start.4 = (s32[32]{0:T(128)S(1)}, s32[32]{0:T(128)}, u32[]{:S(2)}) copy-start(s32[32]{0:T(128)} %param.7) | copy-start | bytes 388
  24.4 27.3 %collective-permute-start = (bf16[256,1024]{1,0:T(8,128)(2,1)S(1)}, bf16[256,1024]{1,0:T(8,128)(2,1)S(1)}, u32[]{:S(2)}, u32[]{:S(2)}) collective-permute-start(bf16[256,1024]{1,0:T(8,128)(2,1)S(1)} %get-tuple-element.6), channel_id=1, source_target_pairs={{0,1},{1,2},{2,3},{3,4},{4,5},{5,6},{6,7},{8,9},{9,10},{10,11},{11... | collective-permute-start | bytes 1572872 | tf_op jit(solution)/shard_map/ppermute | solution.py:17
  29.3 22.4 %collective-permute-start.1 = (bf16[256,1024]{1,0:T(8,128)(2,1)S(1)}, bf16[256,1024]{1,0:T(8,128)(2,1)S(1)}, u32[]{:S(2)}, u32[]{:S(2)}) collective-permute-start(bf16[256,1024]{1,0:T(8,128)(2,1)S(1)} %get-tuple-element.7), channel_id=1, source_target_pairs={{1,0},{2,1},{3,2},{4,3},{5,4},{6,5},{7,6},{9,8},{10,9},{11,10},{12... | collective-permute-start | bytes 1572872 | tf_op jit(solution)/shard_map/ppermute | solution.py:19
  59.8 7.9 %copy-start.1 = (bf16[4096,1024]{1,0:T(8,128)(2,1)}, bf16[4096,1024]{1,0:T(8,128)(2,1)S(1)}, u32[]{:S(2)}) copy-start(bf16[4096,1024]{1,0:T(8,128)(2,1)S(1)} %maximum_select_fusion) | copy-start | bytes 25165828
  216.9 19.8 %copy-start.3 = (f32[64,1024]{1,0:T(8,128)}, f32[64,1024]{1,0:T(8,128)S(1)}, u32[]{:S(2)}) copy-start(f32[64,1024]{1,0:T(8,128)S(1)} %fusion.12) | copy-start | bytes 786436
Sparse Core Ops, SparseCore 0:
  73.1 128.7 all-reduce.4
where the time goes:
time: 244 us
  waiting for transfers between devices  97.8 us (40%)
  blocking collectives  41.8 us (17%)
  matrix products  36.1 us (15%)
  other arithmetic  28.6 us (12%)
  local copies, waits for them, and re-layouts  17 us (7%)
  between operations  16.2 us (7%)
  starting transfers between devices  6.26 us (3%)
    psum x1, waiting for transfers between devices, per_device(): lax.psum((local_update, local_sums, local_count), ('region', 'tile'))  86.2 us
    psum x1, blocking collectives, per_device(): lax.psum((local_update, local_sums, local_count), ('region', 'tile'))  41.8 us
    dot_general x1, matrix products, finish(): lax.dot_general(new_basis, centred, (((0,), (1,)), ((), ())), precision=l...  19.8 us
    ppermute x1, waiting for transfers between devices, padded_2(): lax.ppermute(tail, axis, [(i, (i + 1) % count) for i in range(ends)])  11.5 us
    convert_element_type x1, other arithmetic, dequantize(): return blocks.reshape(tok_rows, feat_dim).astype(jnp.bfloat16)  7.73 us
    slice x1, local copies, waits for them, and re-layouts, per_device(): restored[BAND:tok_rows - BAND]  6.93 us
    dot_general x1, matrix products, per_device(): reduced = jnp.dot(masked_wide, prior_basis, precision=lax.Precision.HIGHEST)  6.67 us
    another operation x3, other arithmetic, finish(): factor = jnp.linalg.cholesky(cross_sum)  6.52 us
  transfers between devices with their start and end apart: 3, of which 2 were waited for; matrix products, arithmetic and copies ran while one was open for 3% of the time, Pallas kernels for 0%

commit v1 on v0

v1 whole, which is shorter than its diff:
```python
import functools

import jax
import jax.numpy as jnp
from jax import lax
from jax.experimental import pallas as pl
from jax.experimental.pallas import tpu as pltpu
from jax.sharding import PartitionSpec as P

BAND = 256
MESH = pl.DeviceIdType.MESH
F32 = jnp.float32
BF16 = jnp.bfloat16
HIGH = lax.Precision.HIGHEST
NT = (((1,), (1,)), ((), ()))
NN = (((1,), (0,)), ((), ()))


def split(value):
    hi = value.astype(BF16)
    lo = (value - hi.astype(F32)).astype(BF16)
    return hi, lo


def kernel(
    n_region, n_tile, owners, width,
    bw_ref, vc_ref, q_ref, sc_ref, p_ref,
    out_ref, basis_ref,
    rows, acc, parts, edge, head_msg, head_got, z_msg, z_got,
    local, extra, got, got_extra, total, total_extra,
    in_sem, m_send, m_recv, z_send, z_recv,
    rs_send, rs_recv, rx_send, rx_recv, ag_send, ag_recv, ax_send, ax_recv,
):
    tokens, feats = rows.shape
    k = p_ref.shape[1]
    count = tokens // BAND
    last = count - 1
    devices = n_region * n_tile
    region, tile = lax.axis_index("region"), lax.axis_index("tile")
    me = region * n_tile + tile
    per_row = feats // width

    def where_is(flat):
        return (lax.div(flat, n_tile), lax.rem(flat, n_tile))

    def span(c):
        return pl.ds(pl.multiple_of(c * BAND, BAND), BAND)

    def fetch(c):
        return pltpu.make_async_copy(q_ref.at[span(c)], rows.at[span(c)], in_sem.at[c])

    fetch(0).start()
    fetch(last).start()

    @pl.loop(1, last)
    def _(c):
        fetch(c).start()

    barrier = pltpu.get_barrier_semaphore()

    @pl.loop(1, devices)
    def _(d):
        pl.semaphore_signal(
            barrier, inc=1, device_id=where_is(lax.rem(me + d, devices)), device_id_type=MESH
        )

    basis_t = p_ref[...].T
    hi, lo = split(basis_t)
    parts[pl.ds(0, k), :] = hi
    parts[pl.ds(k, k), :] = lo
    acc[...] = jnp.zeros_like(acc)

    valid = vc_ref[0]
    left_width = jnp.where(tile > 0, bw_ref[me], 0)
    right_width = jnp.where(tile < n_tile - 1, bw_ref[jnp.minimum(me + 1, devices - 1)], 0)
    place = lax.broadcasted_iota(jnp.int32, (1, BAND), 1)

    def ones(cond):
        return jnp.where(cond, 1.0, 0.0).astype(F32)

    def restore(c):
        fetch(c).wait()
        scale = sc_ref[:, span(c)].T
        step = feats // scale.shape[1]
        for j in range(scale.shape[1]):
            cols = pl.ds(j * step, step)
            rows[span(c), cols] = (
                rows[span(c), cols].astype(F32) * scale[:, j : j + 1]
            ).astype(BF16)

    def project(c):
        both = lax.dot_general(parts[...], rows[span(c), :], NT, preferred_element_type=F32)
        return both[:k] + both[k:]

    def gather_update(c, weighted, weights):
        hi, lo = split(weighted)
        ones_rows = jnp.broadcast_to(weights, (16, BAND)).astype(BF16)
        lhs = jnp.concatenate([hi, lo, ones_rows], axis=0)
        acc[...] += lax.dot_general(lhs, rows[span(c), :], NN, preferred_element_type=F32)

    def to_left(src, dst, send, recv):
        return pltpu.make_async_remote_copy(
            src_ref=src.at[0], dst_ref=dst.at[1], send_sem=send.at[0], recv_sem=recv.at[1],
            device_id=(region, jnp.maximum(tile - 1, 0)), device_id_type=MESH,
        )

    def to_right(src, dst, send, recv):
        return pltpu.make_async_remote_copy(
            src_ref=src.at[1], dst_ref=dst.at[0], send_sem=send.at[1], recv_sem=recv.at[0],
            device_id=(region, jnp.minimum(tile + 1, n_tile - 1)), device_id_type=MESH,
        )

    has_left, has_right = tile > 0, tile < n_tile - 1

    def swap_start(src, dst, send, recv):
        @pl.when(has_left)
        def _():
            to_left(src, dst, send, recv).start()

        @pl.when(has_right)
        def _():
            to_right(src, dst, send, recv).start()

    def swap_wait(src, dst, send, recv):
        @pl.when(has_left)
        def _():
            to_left(src, dst, send, recv).wait_send()
            to_right(src, dst, send, recv).wait_recv()

        @pl.when(has_right)
        def _():
            to_right(src, dst, send, recv).wait_send()
            to_left(src, dst, send, recv).wait_recv()

    @pl.when(tile == 0)
    def _():
        head_got[0] = jnp.zeros(head_got.shape[1:], BF16)
        z_got[0] = jnp.zeros(z_got.shape[1:], BF16)

    @pl.when(tile == n_tile - 1)
    def _():
        head_got[1] = jnp.zeros(head_got.shape[1:], BF16)
        z_got[1] = jnp.zeros(z_got.shape[1:], BF16)

    count_hi = lax.shift_right_logical(valid, 6)
    count_lo = valid - count_hi * 64
    for side, c in ((0, 0), (1, last)):
        restore(c)
        own = project(c)
        edge[side] = own
        hi, lo = split(own)
        head_msg[side, pl.ds(0, k), :] = hi
        head_msg[side, pl.ds(k, k), :] = lo
        head_msg[side, pl.ds(2 * k, 16), :] = jnp.full((16, BAND), count_hi.astype(F32), F32).astype(BF16)
        head_msg[side, pl.ds(2 * k + 16, 16), :] = jnp.full((16, BAND), count_lo.astype(F32), F32).astype(BF16)

    pl.semaphore_wait(barrier, devices - 1)
    swap_start(head_msg, head_got, m_send, m_recv)

    @pl.loop(1, last)
    def _(c):
        restore(c)
        weights = ones(c * BAND + place < valid)
        gather_update(c, project(c) * weights, weights)

    from_row = lax.broadcasted_iota(jnp.int32, (BAND, BAND), 0)
    to_col = lax.broadcasted_iota(jnp.int32, (BAND, BAND), 1)
    shifts = (BAND - left_width, right_width - BAND)
    paired = (place < left_width, place >= BAND - right_width)
    own_valid = (ones(place < valid), ones(tokens - BAND + place < valid))

    def aligned(side, message):
        pick = ones(from_row == to_col + shifts[side]).astype(BF16)
        moved = lax.dot_general(message, pick, NN, preferred_element_type=F32)
        return moved[:k] + moved[k:]

    swap_wait(head_msg, head_got, m_send, m_recv)
    for side, c in ((0, 0), (1, last)):
        other = aligned(side, head_got[side, pl.ds(0, 2 * k), :])
        hi = head_got[side, pl.ds(2 * k, 16), :].astype(F32)
        lo = head_got[side, pl.ds(2 * k + 16, 16), :].astype(F32)
        other_count = (hi * 64.0 + lo)[:1]
        start = tokens - left_width if side == 0 else right_width - BAND
        other_valid = ones((place + start).astype(F32) < other_count)
        both = own_valid[side] + other_valid
        own = edge[side]
        weighted = jnp.where(
            paired[side], (own + other) * (both * 0.25), own * own_valid[side]
        )
        weights = jnp.where(paired[side], both * 0.5, own_valid[side])
        gather_update(c, weighted, weights)

    local[...] = acc[pl.ds(0, k), :] + acc[pl.ds(k, k), :]
    sums = acc[pl.ds(2 * k, 8), :][:1]
    groups = feats // 128
    extra[...] = jnp.concatenate(
        [
            jnp.concatenate([sums[:, i * 128 : (i + 1) * 128] for i in range(groups)], axis=0),
            jnp.full((groups, 128), valid.astype(F32), F32),
        ],
        axis=1,
    )

    def chunk(ref, i):
        return ref.at[
            pl.ds(pl.multiple_of(lax.div(i, per_row) * 8, 8), 8),
            pl.ds(pl.multiple_of(lax.rem(i, per_row) * width, 128), width),
        ]

    def scatter(d):
        target = lax.rem(me + d, devices)
        return pltpu.make_async_remote_copy(
            src_ref=chunk(local, lax.rem(target, owners)), dst_ref=got.at[d - 1],
            send_sem=rs_send.at[d - 1], recv_sem=rs_recv.at[d - 1],
            device_id=where_is(target), device_id_type=MESH,
        )

    def scatter_extra(d):
        return pltpu.make_async_remote_copy(
            src_ref=extra, dst_ref=got_extra.at[d - 1],
            send_sem=rx_send, recv_sem=rx_recv.at[d - 1],
            device_id=where_is(lax.rem(me + d, devices)), device_id_type=MESH,
        )

    def spread(d):
        mine = chunk(total, lax.rem(me, owners))
        return pltpu.make_async_remote_copy(
            src_ref=mine, dst_ref=mine,
            send_sem=ag_send.at[d - 1], recv_sem=ag_recv.at[d - 1],
            device_id=where_is(lax.rem(me + d, devices)), device_id_type=MESH,
        )

    def spread_extra(d):
        return pltpu.make_async_remote_copy(
            src_ref=total_extra, dst_ref=total_extra,
            send_sem=ax_send.at[d - 1], recv_sem=ax_recv,
            device_id=where_is(lax.rem(me + d, devices)), device_id_type=MESH,
        )

    @pl.when(me != 0)
    def _():
        scatter_extra(devices - me).start()

    @pl.loop(1, devices)
    def _(d):
        @pl.when(lax.rem(me + d, devices) < owners)
        def _():
            scatter(d).start()

    @pl.when(me == 0)
    def _():
        @pl.loop(1, devices)
        def _(d):
            scatter_extra(d).wait_recv()

        def add(d, so_far):
            return so_far + got_extra[d]

        total_extra[...] = lax.fori_loop(0, devices - 1, add, extra[...])

        @pl.loop(1, devices)
        def _(d):
            spread_extra(d).start()

    @pl.when(me < owners)
    def _():
        @pl.loop(1, devices)
        def _(d):
            scatter(d).wait_recv()

        def add(d, so_far):
            return so_far + got[d]

        chunk(total, lax.rem(me, owners))[...] = lax.fori_loop(
            0, devices - 1, add, chunk(local, lax.rem(me, owners))[...]
        )

        @pl.loop(1, devices)
        def _(d):
            spread(d).start()

    @pl.when(me != 0)
    def _():
        spread_extra(1).wait_recv()

    @pl.loop(1, devices)
    def _(d):
        @pl.when(lax.rem(me + devices - d, devices) < owners)
        def _():
            spread(d).wait_recv()

    packed = total_extra[...]
    token_count = packed[:1, 128:129]
    sums = jnp.concatenate([packed[i : i + 1, :128] for i in range(groups)], axis=1)
    average = sums / token_count
    mean_image = jnp.sum(p_ref[...].T * average, axis=1, keepdims=True)
    update = total[...] - mean_image * sums
    cross = lax.dot_general(update, update, NT, precision=HIGH, preferred_element_type=F32)
    row = lax.broadcasted_iota(jnp.int32, (k, k), 0)
    col = lax.broadcasted_iota(jnp.int32, (k, k), 1)
    work = jnp.concatenate([cross, ones(row == col)], axis=1)
    line = lax.broadcasted_iota(jnp.int32, (k, 1), 0)
    for i in range(k - 1):
        pivot = work[i : i + 1, :]
        scaled = pivot * (1.0 / pivot[:, i : i + 1])
        work = work - jnp.where(line > i, work[:, i : i + 1], 0.0) * scaled
    diagonal = jnp.sum(jnp.where(row == col, work[:, :k], 0.0), axis=1, keepdims=True)
    inverse = work[:, k:] / jnp.sqrt(diagonal)
    new_t = lax.dot_general(inverse, update, NN, precision=HIGH, preferred_element_type=F32)
    basis_ref[...] = new_t.T
    shift = jnp.sum(new_t * average, axis=1, keepdims=True)
    hi, lo = split(new_t)
    parts[pl.ds(0, k), :] = hi
    parts[pl.ds(k, k), :] = lo

    for side, c in ((0, 0), (1, last)):
        own = project(c)
        edge[side] = own
        hi, lo = split(own)
        z_msg[side, pl.ds(0, k), :] = hi
        z_msg[side, pl.ds(k, k), :] = lo
    swap_start(z_msg, z_got, z_send, z_recv)

    @pl.loop(1, last)
    def _(c):
        usable = c * BAND + place < valid
        out_ref[:, span(c)] = jnp.where(usable, project(c) - shift, 0.0)

    swap_wait(z_msg, z_got, z_send, z_recv)
    for side, c in ((0, 0), (1, last)):
        other = aligned(side, z_got[side])
        own = edge[side]
        mixed = jnp.where(paired[side], (own + other) * 0.5, own)
        out_ref[:, span(c)] = jnp.where(own_valid[side] > 0.5, mixed - shift, 0.0)

    @pl.when(me != 0)
    def _():
        scatter_extra(devices - me).wait_send()

    @pl.when(me == 0)
    def _():
        @pl.loop(1, devices)
        def _(d):
            spread_extra(d).wait_send()

    @pl.when(me < owners)
    def _():
        @pl.loop(1, devices)
        def _(d):
            spread(d).wait_send()

    @pl.loop(1, devices)
    def _(d):
        @pl.when(lax.rem(me + d, devices) < owners)
        def _():
            scatter(d).wait_send()


def per_device(n_region, n_tile, quantized, block_scales, band_width, valid_count, prior_basis):
    tokens, feats = quantized.shape
    k = prior_basis.shape[1]
    devices = n_region * n_tile
    tiles = (k // 8) * (feats // 128)
    owners = min(devices, tiles)
    width = 128 * (tiles // owners)
    others = devices - 1
    dma = pltpu.SemaphoreType.DMA
    vmem = pl.BlockSpec(memory_space=pltpu.VMEM)
    smem = pl.BlockSpec(memory_space=pltpu.SMEM)
    return pl.pallas_call(
        functools.partial(kernel, n_region, n_tile, owners, width),
        out_shape=(
            jax.ShapeDtypeStruct((k, tokens), F32),
            jax.ShapeDtypeStruct((feats, k), F32),
        ),
        in_specs=[smem, smem, pl.BlockSpec(memory_space=pl.ANY), vmem, vmem],
        out_specs=(vmem, vmem),
        scratch_shapes=[
            pltpu.VMEM((tokens, feats), BF16),
            pltpu.VMEM((2 * k + 16, feats), F32),
            pltpu.VMEM((2 * k, feats), BF16),
            pltpu.VMEM((2, k, BAND), F32),
            pltpu.VMEM((2, 2 * k + 32, BAND), BF16),
            pltpu.VMEM((2, 2 * k + 32, BAND), BF16),
            pltpu.VMEM((2, 2 * k, BAND), BF16),
            pltpu.VMEM((2, 2 * k, BAND), BF16),
            pltpu.VMEM((k, feats), F32),
            pltpu.VMEM((feats // 128, 256), F32),
            pltpu.VMEM((others, 8, width), F32),
            pltpu.VMEM((others, feats // 128, 256), F32),
            pltpu.VMEM((k, feats), F32),
            pltpu.VMEM((feats // 128, 256), F32),
            dma((tokens // BAND,)),
            dma((2,)), dma((2,)), dma((2,)), dma((2,)),
            dma((others,)), dma((others,)), dma(()), dma((others,)),
            dma((others,)), dma((others,)), dma((others,)), dma(()),
        ],
        compiler_params=pltpu.CompilerParams(
            collective_id=0, has_side_effects=True, vmem_limit_bytes=48 * 1024 * 1024
        ),
    )(band_width, valid_count, quantized, block_scales, prior_basis)


def solution(mesh):
    return jax.shard_map(
        functools.partial(per_device, mesh.shape["region"], mesh.shape["tile"]),
        mesh=mesh,
        in_specs=(
            P(("region", "tile"), None),
            P(None, ("region", "tile")),
            P(),
            P(("region", "tile")),
            P(),
        ),
        out_specs=(P(None, ("region", "tile")), P()),
        check_vma=False,
    )
```

time: 244 us -> 59.3 us (0.24)
  waiting for transfers between devices: 97.8 us -> 0 us
  Pallas kernels: 0 us -> 53.2 us
  blocking collectives: 41.8 us -> 0 us
  matrix products: 36.1 us -> 0 us
  other arithmetic: 28.6 us -> 0 us
  between operations: 16.2 us -> 1.3 us
  local copies, waits for them, and re-layouts: 17 us -> 4.56 us
  starting transfers between devices: 6.26 us -> 0 us
    psum x1 -> x0, waiting for transfers between devices: 86.2 us -> none  [per_device(): lax.psum((local_update, local_sums, local_count), ('region', 'tile'))]
    pallas_call x0 -> x1, Pallas kernels: none -> 53.2 us  [per_device(): pl.pallas_call(functools.partial(kernel, n_region, n_tile, owners, width)...]
    psum x1 -> x0, blocking collectives: 41.8 us -> none  [per_device(): lax.psum((local_update, local_sums, local_count), ('region', 'tile'))]
    dot_general x6 -> x0, matrix products: 34.6 us -> none  [the longest x1 19.8 us: finish(): lax.dot_general(new_basis, centred, (((0,), (1,)), ((), ())), precision=l...]
    another operation x5 -> x0, other arithmetic: 12.1 us -> none  [the longest x3 6.52 us: finish(): factor = jnp.linalg.cholesky(cross_sum)]
    ppermute x2 -> x0, waiting for transfers between devices: 11.5 us -> none  [the longest x1 11.5 us: padded_2(): lax.ppermute(tail, axis, [(i, (i + 1) % count) for i in range(ends)])]
    convert_element_type x2 -> x0, other arithmetic: 9.58 us -> none  [the longest x1 7.73 us: dequantize(): return blocks.reshape(tok_rows, feat_dim).astype(jnp.bfloat16)]
    slice x2 -> x0, local copies, waits for them, and re-layouts: 7 us -> none  [the longest x1 6.93 us: per_device(): restored[BAND:tok_rows - BAND]]
  transfers between devices with their start and end apart: 3 -> 0, of which waited for: 2 -> 0; matrix products, arithmetic and copies ran while one was open for 3% -> 0% of each run, Pallas kernels for 0% -> 0%
where the time goes in v1:
time: 59.3 us; the launch traced here: 59.1 us
  Pallas kernels  53.2 us (90%)
  local copies, waits for them, and re-layouts  4.56 us (8%)
  between operations  1.3 us (2%)
    pallas_call x1, Pallas kernels, per_device(): pl.pallas_call(functools.partial(kernel, n_region, n_tile, owners, width)...  53.2 us
    unnamed x6, local copies, waits for them, and re-layouts  3.67 us

profile of v1, /device:TPU:0, one launch (start us, length us, event | category | flops | bytes accessed | tf_op | source)
XLA Modules:
  0.0 59.1 jit_solution(14658709822806935587)
XLA Ops:
  1.3 1.1 %copy.7.p_ref = f32[1024,64]{1,0:T(8,128)S(1)} copy(f32[1024,64]{0,1:T(8,128)} %param.9) | data formatting | bytes 524288 | tf_op args[4]
  2.4 0.0 copy-start
  2.4 0.9 %copy-done = f32[8,4096]{1,0:T(8,128)S(1)} copy-done((f32[8,4096]{1,0:T(8,128)S(1)}, f32[8,4096]{1,0:T(8,128)}, u32[]{:S(2)}) %copy-start) | copy-done | bytes 131096
  3.3 0.0 copy-start.1
  3.3 0.7 %copy-done.1 = s32[32]{0:T(128)S(1)} copy-done((s32[32]{0:T(128)S(1)}, s32[32]{0:T(128)}, u32[]{:S(2)}) %copy-start.1) | copy-done | bytes 152
  4.0 53.2 %shard_map.68 = (f32[64,4096]{1,0:T(8,128)S(1)}, f32[1024,64]{1,0:T(8,128)S(1)}) custom-call(s32[32]{0:T(128)S(1)} %copy-done.1, s32[1]{0:T(128)S(6)} %copy.10.vc_ref, bf16[4096,1024]{1,0:T(8,128)(2,1)} %q_ref.1, f32[8,4096]{1,0:T(8,128)S(1)} %copy-done, f32[1024,64]{1,0:T(8,128)S(1)} %copy.7.p_ref), custom_call_target="tpu_custom_call" | custom-call | tf_op jit(solution)/shard_map/pallas_call | solution.py:370
  57.2 0.9 %copy.8 = f32[1024,64]{0,1:T(8,128)} copy(f32[1024,64]{1,0:T(8,128)S(1)} %get-tuple-element.3) | data formatting | bytes 524288 | tf_op jit(solution)/shard_map/pallas_call | solution.py:370
  58.1 1.0 %copy.11 = f32[64,4096]{1,0:T(8,128)} copy(f32[64,4096]{1,0:T(8,128)S(1)} %get-tuple-element.6) | data formatting | bytes 2097152
Async XLA Ops:
  2.4 0.9 %copy-start = (f32[8,4096]{1,0:T(8,128)S(1)}, f32[8,4096]{1,0:T(8,128)}, u32[]{:S(2)}) copy-start(f32[8,4096]{1,0:T(8,128)} %sc_ref.1) | copy-start | bytes 393220
  3.3 0.7 %copy-start.1 = (s32[32]{0:T(128)S(1)}, s32[32]{0:T(128)}, u32[]{:S(2)}) copy-start(s32[32]{0:T(128)} %bw_ref.1) | copy-start | bytes 388

commit v2 on v1

--- a/solution.py
+++ b/solution.py
@@ -24,15 +24,15 @@
 
 def kernel(
     n_region, n_tile, owners, width,
-    bw_ref, vc_ref, q_ref, sc_ref, p_ref,
+    bw_ref, vc_ref, q_ref, sc_hbm, p_hbm,
     out_ref, basis_ref,
-    rows, acc, parts, edge, head_msg, head_got, z_msg, z_got,
+    rows, sc_ref, p_ref, acc, parts, edge, head_msg, head_got, z_msg, z_got,
     local, extra, got, got_extra, total, total_extra,
-    in_sem, m_send, m_recv, z_send, z_recv,
+    in_sem, small_sem, m_send, m_recv, z_send, z_recv,
     rs_send, rs_recv, rx_send, rx_recv, ag_send, ag_recv, ax_send, ax_recv,
 ):
     tokens, feats = rows.shape
-    k = p_ref.shape[1]
+    k = p_ref.shape[0]
     count = tokens // BAND
     last = count - 1
     devices = n_region * n_tile
@@ -44,11 +44,19 @@
         return (lax.div(flat, n_tile), lax.rem(flat, n_tile))
 
     def span(c):
+        if isinstance(c, int):
+            return pl.ds(c * BAND, BAND)
         return pl.ds(pl.multiple_of(c * BAND, BAND), BAND)
 
     def fetch(c):
         return pltpu.make_async_copy(q_ref.at[span(c)], rows.at[span(c)], in_sem.at[c])
 
+    def fetch_small(i):
+        source, target = ((sc_hbm, sc_ref), (p_hbm, p_ref))[i]
+        return pltpu.make_async_copy(source, target, small_sem.at[i])
+
+    fetch_small(1).start()
+    fetch_small(0).start()
     fetch(0).start()
     fetch(last).start()
 
@@ -64,8 +72,8 @@
             barrier, inc=1, device_id=where_is(lax.rem(me + d, devices)), device_id_type=MESH
         )
 
-    basis_t = p_ref[...].T
-    hi, lo = split(basis_t)
+    fetch_small(1).wait()
+    hi, lo = split(p_ref[...])
     parts[pl.ds(0, k), :] = hi
     parts[pl.ds(k, k), :] = lo
     acc[...] = jnp.zeros_like(acc)
@@ -78,24 +86,32 @@
     def ones(cond):
         return jnp.where(cond, 1.0, 0.0).astype(F32)
 
+    blocks = sc_ref.shape[0]
+    step = feats // blocks
+
+    def restore_block(c, scale, j):
+        cols = pl.ds(j * step, step)
+        rows[span(c), cols] = (
+            rows[span(c), cols].astype(F32) * scale[:, j : j + 1]
+        ).astype(BF16)
+
     def restore(c):
         fetch(c).wait()
         scale = sc_ref[:, span(c)].T
-        step = feats // scale.shape[1]
-        for j in range(scale.shape[1]):
-            cols = pl.ds(j * step, step)
-            rows[span(c), cols] = (
-                rows[span(c), cols].astype(F32) * scale[:, j : j + 1]
-            ).astype(BF16)
+        for j in range(blocks):
+            restore_block(c, scale, j)
 
     def project(c):
         both = lax.dot_general(parts[...], rows[span(c), :], NT, preferred_element_type=F32)
         return both[:k] + both[k:]
 
-    def gather_update(c, weighted, weights):
+    def left_side(weighted, weights):
         hi, lo = split(weighted)
         ones_rows = jnp.broadcast_to(weights, (16, BAND)).astype(BF16)
-        lhs = jnp.concatenate([hi, lo, ones_rows], axis=0)
+        return jnp.concatenate([hi, lo, ones_rows], axis=0)
+
+    def gather_update(c, weighted, weights):
+        lhs = left_side(weighted, weights)
         acc[...] += lax.dot_general(lhs, rows[span(c), :], NN, preferred_element_type=F32)
 
     def to_left(src, dst, send, recv):
@@ -142,6 +158,7 @@
         head_got[1] = jnp.zeros(head_got.shape[1:], BF16)
         z_got[1] = jnp.zeros(z_got.shape[1:], BF16)
 
+    fetch_small(0).wait()
     count_hi = lax.shift_right_logical(valid, 6)
     count_lo = valid - count_hi * 64
     for side, c in ((0, 0), (1, last)):
@@ -157,11 +174,29 @@
     pl.semaphore_wait(barrier, devices - 1)
     swap_start(head_msg, head_got, m_send, m_recv)
 
-    @pl.loop(1, last)
-    def _(c):
-        restore(c)
+    restore(1)
+    pieces = blocks // 2
+    for c in range(1, last):
+        following = c + 1 < last
+        if following:
+            fetch(c + 1).wait()
+            scale = sc_ref[:, span(c + 1)].T
         weights = ones(c * BAND + place < valid)
-        gather_update(c, project(c) * weights, weights)
+        weighted = project(c) * weights
+        if following:
+            for j in range(pieces):
+                restore_block(c + 1, scale, j)
+        lhs = left_side(weighted, weights)
+        for j in range(pieces):
+            cols = pl.ds(j * (feats // pieces), feats // pieces)
+            acc[:, cols] += lax.dot_general(
+                lhs, rows[span(c), cols], NN, preferred_element_type=F32
+            )
+            if following and pieces + j < blocks:
+                restore_block(c + 1, scale, pieces + j)
+        if following:
+            for j in range(2 * pieces, blocks):
+                restore_block(c + 1, scale, j)
 
     from_row = lax.broadcasted_iota(jnp.int32, (BAND, BAND), 0)
     to_col = lax.broadcasted_iota(jnp.int32, (BAND, BAND), 1)
@@ -293,21 +328,30 @@
     token_count = packed[:1, 128:129]
     sums = jnp.concatenate([packed[i : i + 1, :128] for i in range(groups)], axis=1)
     average = sums / token_count
-    mean_image = jnp.sum(p_ref[...].T * average, axis=1, keepdims=True)
+    mean_image = jnp.sum(p_ref[...] * average, axis=1, keepdims=True)
     update = total[...] - mean_image * sums
     cross = lax.dot_general(update, update, NT, precision=HIGH, preferred_element_type=F32)
     row = lax.broadcasted_iota(jnp.int32, (k, k), 0)
     col = lax.broadcasted_iota(jnp.int32, (k, k), 1)
     work = jnp.concatenate([cross, ones(row == col)], axis=1)
     line = lax.broadcasted_iota(jnp.int32, (k, 1), 0)
-    for i in range(k - 1):
-        pivot = work[i : i + 1, :]
-        scaled = pivot * (1.0 / pivot[:, i : i + 1])
-        work = work - jnp.where(line > i, work[:, i : i + 1], 0.0) * scaled
+    group = 4
+    for first in range(0, k, group):
+        wide = [
+            jnp.broadcast_to(work[:, i : i + 1], (k, 2 * k))
+            for i in range(first, first + group)
+        ]
+        for j in range(group):
+            i = first + j
+            below = jnp.where(line > i, wide[j], 0.0)
+            turn = 1.0 / wide[j][i : i + 1, :]
+            for l in range(j + 1, group):
+                wide[l] = wide[l] - below * (wide[l][i : i + 1, :] * turn)
+            work = work - below * (work[i : i + 1, :] * turn)
     diagonal = jnp.sum(jnp.where(row == col, work[:, :k], 0.0), axis=1, keepdims=True)
     inverse = work[:, k:] / jnp.sqrt(diagonal)
     new_t = lax.dot_general(inverse, update, NN, precision=HIGH, preferred_element_type=F32)
-    basis_ref[...] = new_t.T
+    basis_ref[...] = new_t
     shift = jnp.sum(new_t * average, axis=1, keepdims=True)
     hi, lo = split(new_t)
     parts[pl.ds(0, k), :] = hi
@@ -367,16 +411,18 @@
     dma = pltpu.SemaphoreType.DMA
     vmem = pl.BlockSpec(memory_space=pltpu.VMEM)
     smem = pl.BlockSpec(memory_space=pltpu.SMEM)
-    return pl.pallas_call(
+    projected, basis = pl.pallas_call(
         functools.partial(kernel, n_region, n_tile, owners, width),
         out_shape=(
             jax.ShapeDtypeStruct((k, tokens), F32),
-            jax.ShapeDtypeStruct((feats, k), F32),
+            jax.ShapeDtypeStruct((k, feats), F32),
         ),
-        in_specs=[smem, smem, pl.BlockSpec(memory_space=pl.ANY), vmem, vmem],
+        in_specs=[smem, smem] + [pl.BlockSpec(memory_space=pltpu.HBM)] * 3,
         out_specs=(vmem, vmem),
         scratch_shapes=[
             pltpu.VMEM((tokens, feats), BF16),
+            pltpu.VMEM(block_scales.shape, F32),
+            pltpu.VMEM((k, feats), F32),
             pltpu.VMEM((2 * k + 16, feats), F32),
             pltpu.VMEM((2 * k, feats), BF16),
             pltpu.VMEM((2, k, BAND), F32),
@@ -390,7 +436,7 @@
             pltpu.VMEM((others, feats // 128, 256), F32),
             pltpu.VMEM((k, feats), F32),
             pltpu.VMEM((feats // 128, 256), F32),
-            dma((tokens // BAND,)),
+            dma((tokens // BAND,)), dma((2,)),
             dma((2,)), dma((2,)), dma((2,)), dma((2,)),
             dma((others,)), dma((others,)), dma(()), dma((others,)),
             dma((others,)), dma((others,)), dma((others,)), dma(()),
@@ -398,7 +444,8 @@
         compiler_params=pltpu.CompilerParams(
             collective_id=0, has_side_effects=True, vmem_limit_bytes=48 * 1024 * 1024
         ),
-    )(band_width, valid_count, quantized, block_scales, prior_basis)
+    )(band_width, valid_count, quantized, block_scales, prior_basis.T)
+    return projected, basis.T
 
 
 def solution(mesh):

time: 59.3 us -> 49.3 us (0.83)
  Pallas kernels: 53.2 us -> 43.7 us
    pallas_call x1, Pallas kernels: 53.2 us -> 43.7 us  [per_device(): pl.pallas_call(functools.partial(kernel, n_region, n_tile, owners, width)...]
    pallas_call x1 -> x0, local copies, waits for them, and re-layouts: 0.89 us -> none  [per_device(): pl.pallas_call(functools.partial(kernel, n_region, n_tile, owners, width)...]
    unnamed x6 -> x8, local copies, waits for them, and re-layouts: 3.67 us -> 4.18 us
where the time goes in v2:
time: 49.3 us; the launch traced here: 49.2 us
  Pallas kernels  43.7 us (89%)
  local copies, waits for them, and re-layouts  4.18 us (8%)
  between operations  1.3 us (3%)
    pallas_call x1, Pallas kernels, per_device(): pl.pallas_call(functools.partial(kernel, n_region, n_tile, owners, width)...  43.7 us
    unnamed x8, local copies, waits for them, and re-layouts  4.18 us

profile of v2, /device:TPU:0, one launch (start us, length us, event | category | flops | bytes accessed | tf_op | source)
XLA Modules:
  0.0 49.2 jit_solution(3080120263540681409)
XLA Ops:
  1.3 0.0 copy-start
  1.3 0.9 %copy-done = f32[1024,64]{0,1:T(8,128)S(1)} copy-done((f32[1024,64]{0,1:T(8,128)S(1)}, f32[1024,64]{0,1:T(8,128)}, u32[]{:S(2)}) %copy-start) | copy-done | bytes 262168
  2.2 0.0 copy-start.1
  2.2 0.9 %copy-done.1 = f32[8,4096]{1,0:T(8,128)S(1)} copy-done((f32[8,4096]{1,0:T(8,128)S(1)}, f32[8,4096]{1,0:T(8,128)}, u32[]{:S(2)}) %copy-start.1) | copy-done | bytes 131096
  3.1 0.0 copy-start.2
  3.1 0.7 %copy-done.2 = s32[32]{0:T(128)S(1)} copy-done((s32[32]{0:T(128)S(1)}, s32[32]{0:T(128)}, u32[]{:S(2)}) %copy-start.2) | copy-done | bytes 152
  3.8 43.7 %shard_map.68 = (f32[64,4096]{1,0:T(8,128)S(1)}, f32[64,1024]{1,0:T(8,128)S(1)}) custom-call(s32[32]{0:T(128)S(1)} %copy-done.2, s32[1]{0:T(128)S(6)} %copy.9.vc_ref, bf16[4096,1024]{1,0:T(8,128)(2,1)} %q_ref.1, f32[8,4096]{1,0:T(8,128)S(1)} %copy-done.1, f32[64,1024]{1,0:T(8,128)S(1)} %bitcast.2), custom_call_target="tpu_custom_call" | custom-call | tf_op jit(solution)/shard_map/pallas_call | solution.py:414
  47.5 1.0 %copy.10 = f32[64,4096]{1,0:T(8,128)} copy(f32[64,4096]{1,0:T(8,128)S(1)} %get-tuple-element.8) | data formatting | bytes 2097152
  48.5 0.7 %copy.11 = f32[1024,64]{0,1:T(8,128)} copy(f32[1024,64]{0,1:T(8,128)S(1)} %bitcast.3) | data formatting | bytes 524288
Async XLA Ops:
  1.3 1.0 %copy-start = (f32[1024,64]{0,1:T(8,128)S(1)}, f32[1024,64]{0,1:T(8,128)}, u32[]{:S(2)}) copy-start(f32[1024,64]{0,1:T(8,128)} %param.9) | copy-start | bytes 786436
  2.2 0.9 %copy-start.1 = (f32[8,4096]{1,0:T(8,128)S(1)}, f32[8,4096]{1,0:T(8,128)}, u32[]{:S(2)}) copy-start(f32[8,4096]{1,0:T(8,128)} %sc_hbm.1) | copy-start | bytes 393220
  3.1 0.7 %copy-start.2 = (s32[32]{0:T(128)S(1)}, s32[32]{0:T(128)}, u32[]{:S(2)}) copy-start(s32[32]{0:T(128)} %bw_ref.1) | copy-start | bytes 388

commit v3 on v2

--- a/solution.py
+++ b/solution.py
@@ -25,10 +25,11 @@
 def kernel(
     n_region, n_tile, owners, width,
     bw_ref, vc_ref, q_ref, sc_hbm, p_hbm,
-    out_ref, basis_ref,
+    out_hbm, basis_ref,
+    out_ref,
     rows, sc_ref, p_ref, acc, parts, edge, head_msg, head_got, z_msg, z_got,
     local, extra, got, got_extra, total, total_extra,
-    in_sem, small_sem, m_send, m_recv, z_send, z_recv,
+    in_sem, small_sem, out_sem, m_send, m_recv, z_send, z_recv,
     rs_send, rs_recv, rx_send, rx_recv, ag_send, ag_recv, ax_send, ax_recv,
 ):
     tokens, feats = rows.shape
@@ -64,6 +65,11 @@
     def _(c):
         fetch(c).start()
 
+    def put(c):
+        return pltpu.make_async_copy(
+            out_ref.at[:, span(c)], out_hbm.at[:, span(c)], out_sem.at[c]
+        )
+
     barrier = pltpu.get_barrier_semaphore()
 
     @pl.loop(1, devices)
@@ -161,42 +167,47 @@
     fetch_small(0).wait()
     count_hi = lax.shift_right_logical(valid, 6)
     count_lo = valid - count_hi * 64
-    for side, c in ((0, 0), (1, last)):
-        restore(c)
-        own = project(c)
+    def send_edge(side, own):
         edge[side] = own
         hi, lo = split(own)
+        whole = (16, BAND)
         head_msg[side, pl.ds(0, k), :] = hi
         head_msg[side, pl.ds(k, k), :] = lo
-        head_msg[side, pl.ds(2 * k, 16), :] = jnp.full((16, BAND), count_hi.astype(F32), F32).astype(BF16)
-        head_msg[side, pl.ds(2 * k + 16, 16), :] = jnp.full((16, BAND), count_lo.astype(F32), F32).astype(BF16)
-
-    pl.semaphore_wait(barrier, devices - 1)
-    swap_start(head_msg, head_got, m_send, m_recv)
-
-    restore(1)
+        head_msg[side, pl.ds(2 * k, 16), :] = jnp.full(whole, count_hi.astype(F32), F32).astype(BF16)
+        head_msg[side, pl.ds(2 * k + 16, 16), :] = jnp.full(whole, count_lo.astype(F32), F32).astype(BF16)
+
+    restore(0)
     pieces = blocks // 2
-    for c in range(1, last):
-        following = c + 1 < last
-        if following:
-            fetch(c + 1).wait()
-            scale = sc_ref[:, span(c + 1)].T
+    order = [0, last] + list(range(1, last))
+    for at, c in enumerate(order):
+        following = order[at + 1] if at + 1 < count else None
+        if following is not None:
+            fetch(following).wait()
+            scale = sc_ref[:, span(following)].T
+        own = project(c)
+        if c in (0, last):
+            for j in range(blocks):
+                restore_block(following, scale, j)
+            send_edge(0 if c == 0 else 1, own)
+            if c == last:
+                pl.semaphore_wait(barrier, devices - 1)
+                swap_start(head_msg, head_got, m_send, m_recv)
+            continue
         weights = ones(c * BAND + place < valid)
-        weighted = project(c) * weights
-        if following:
+        if following is not None:
             for j in range(pieces):
-                restore_block(c + 1, scale, j)
-        lhs = left_side(weighted, weights)
+                restore_block(following, scale, j)
+        lhs = left_side(own * weights, weights)
         for j in range(pieces):
             cols = pl.ds(j * (feats // pieces), feats // pieces)
             acc[:, cols] += lax.dot_general(
                 lhs, rows[span(c), cols], NN, preferred_element_type=F32
             )
-            if following and pieces + j < blocks:
-                restore_block(c + 1, scale, pieces + j)
-        if following:
+            if following is not None:
+                restore_block(following, scale, pieces + j)
+        if following is not None:
             for j in range(2 * pieces, blocks):
-                restore_block(c + 1, scale, j)
+                restore_block(following, scale, j)
 
     from_row = lax.broadcasted_iota(jnp.int32, (BAND, BAND), 0)
     to_col = lax.broadcasted_iota(jnp.int32, (BAND, BAND), 1)
@@ -369,6 +380,7 @@
     def _(c):
         usable = c * BAND + place < valid
         out_ref[:, span(c)] = jnp.where(usable, project(c) - shift, 0.0)
+        put(c).start()
 
     swap_wait(z_msg, z_got, z_send, z_recv)
     for side, c in ((0, 0), (1, last)):
@@ -376,6 +388,7 @@
         own = edge[side]
         mixed = jnp.where(paired[side], (own + other) * 0.5, own)
         out_ref[:, span(c)] = jnp.where(own_valid[side] > 0.5, mixed - shift, 0.0)
+        put(c).start()
 
     @pl.when(me != 0)
     def _():
@@ -398,6 +411,10 @@
         @pl.when(lax.rem(me + d, devices) < owners)
         def _():
             scatter(d).wait_send()
+
+    @pl.loop(0, count)
+    def _(c):
+        put(c).wait()
 
 
 def per_device(n_region, n_tile, quantized, block_scales, band_width, valid_count, prior_basis):
@@ -418,8 +435,9 @@
             jax.ShapeDtypeStruct((k, feats), F32),
         ),
         in_specs=[smem, smem] + [pl.BlockSpec(memory_space=pltpu.HBM)] * 3,
-        out_specs=(vmem, vmem),
+        out_specs=(pl.BlockSpec(memory_space=pl.ANY), vmem),
         scratch_shapes=[
+            pltpu.VMEM((k, tokens), F32),
             pltpu.VMEM((tokens, feats), BF16),
             pltpu.VMEM(block_scales.shape, F32),
             pltpu.VMEM((k, feats), F32),
@@ -436,13 +454,13 @@
             pltpu.VMEM((others, feats // 128, 256), F32),
             pltpu.VMEM((k, feats), F32),
             pltpu.VMEM((feats // 128, 256), F32),
-            dma((tokens // BAND,)), dma((2,)),
+            dma((tokens // BAND,)), dma((2,)), dma((tokens // BAND,)),
             dma((2,)), dma((2,)), dma((2,)), dma((2,)),
             dma((others,)), dma((others,)), dma(()), dma((others,)),
             dma((others,)), dma((others,)), dma((others,)), dma(()),
         ],
         compiler_params=pltpu.CompilerParams(
-            collective_id=0, has_side_effects=True, vmem_limit_bytes=48 * 1024 * 1024
+            collective_id=0, has_side_effects=True, vmem_limit_bytes=67043328
         ),
     )(band_width, valid_count, quantized, block_scales, prior_basis.T)
     return projected, basis.T

time: 49.3 us -> 49.5 us (level)
    unnamed x8 -> x2, local copies, waits for them, and re-layouts: 4.18 us -> 3.94 us
where the time goes in v3:
time: 49.5 us; the launch traced here: 49.3 us
  Pallas kernels  44.1 us (89%)
  local copies, waits for them, and re-layouts  3.94 us (8%)
  between operations  1.29 us (3%)
    pallas_call x1, Pallas kernels, per_device(): pl.pallas_call(functools.partial(kernel, n_region, n_tile, owners, width)...  44.1 us
    unnamed x2, local copies, waits for them, and re-layouts  3.94 us

profile of v3, /device:TPU:0, one launch (start us, length us, event | category | flops | bytes accessed | tf_op | source)
XLA Modules:
  0.0 49.3 jit_solution(14181658513356760073)
XLA Ops:
  1.3 44.1 %shard_map.68 = (f32[64,4096]{1,0:T(8,128)}, f32[64,1024]{1,0:T(8,128)}) custom-call(s32[32]{0:T(128)} %bw_ref.1, s32[1]{0:T(128)S(6)} %copy.9.vc_ref, bf16[4096,1024]{1,0:T(8,128)(2,1)} %q_ref.1, f32[8,4096]{1,0:T(8,128)} %sc_hbm.1, f32[64,1024]{1,0:T(8,128)} %bitcast.2), custom_call_target="tpu_custom_call" | custom-call | tf_op jit(solution)/shard_map/pallas_call | solution.py:431
  45.4 2.3 %copy.10 = f32[64,4096]{1,0:T(8,128)} copy(f32[64,4096]{1,0:T(8,128)} %get-tuple-element.8) | data formatting | bytes 2097152
  47.7 1.7 %copy.11 = f32[1024,64]{0,1:T(8,128)} copy(f32[1024,64]{0,1:T(8,128)} %bitcast.3) | data formatting | bytes 524288

commit v4 on v3

--- a/solution.py
+++ b/solution.py
@@ -24,12 +24,11 @@
 
 def kernel(
     n_region, n_tile, owners, width,
-    bw_ref, vc_ref, q_ref, sc_hbm, p_hbm,
-    out_hbm, basis_ref,
-    out_ref,
-    rows, sc_ref, p_ref, acc, parts, edge, head_msg, head_got, z_msg, z_got,
+    bw_ref, vc_ref, q_ref, sc_ref, p_ref,
+    out_ref, basis_ref,
+    rows, acc, parts, edge, head_msg, head_got, z_msg, z_got,
     local, extra, got, got_extra, total, total_extra,
-    in_sem, small_sem, out_sem, m_send, m_recv, z_send, z_recv,
+    in_sem, m_send, m_recv, z_send, z_recv,
     rs_send, rs_recv, rx_send, rx_recv, ag_send, ag_recv, ax_send, ax_recv,
 ):
     tokens, feats = rows.shape
@@ -52,23 +51,12 @@
     def fetch(c):
         return pltpu.make_async_copy(q_ref.at[span(c)], rows.at[span(c)], in_sem.at[c])
 
-    def fetch_small(i):
-        source, target = ((sc_hbm, sc_ref), (p_hbm, p_ref))[i]
-        return pltpu.make_async_copy(source, target, small_sem.at[i])
-
-    fetch_small(1).start()
-    fetch_small(0).start()
     fetch(0).start()
     fetch(last).start()
 
     @pl.loop(1, last)
     def _(c):
         fetch(c).start()
-
-    def put(c):
-        return pltpu.make_async_copy(
-            out_ref.at[:, span(c)], out_hbm.at[:, span(c)], out_sem.at[c]
-        )
 
     barrier = pltpu.get_barrier_semaphore()
 
@@ -78,7 +66,6 @@
             barrier, inc=1, device_id=where_is(lax.rem(me + d, devices)), device_id_type=MESH
         )
 
-    fetch_small(1).wait()
     hi, lo = split(p_ref[...])
     parts[pl.ds(0, k), :] = hi
     parts[pl.ds(k, k), :] = lo
@@ -164,7 +151,6 @@
         head_got[1] = jnp.zeros(head_got.shape[1:], BF16)
         z_got[1] = jnp.zeros(z_got.shape[1:], BF16)
 
-    fetch_small(0).wait()
     count_hi = lax.shift_right_logical(valid, 6)
     count_lo = valid - count_hi * 64
     def send_edge(side, own):
@@ -380,7 +366,6 @@
     def _(c):
         usable = c * BAND + place < valid
         out_ref[:, span(c)] = jnp.where(usable, project(c) - shift, 0.0)
-        put(c).start()
 
     swap_wait(z_msg, z_got, z_send, z_recv)
     for side, c in ((0, 0), (1, last)):
@@ -388,7 +373,6 @@
         own = edge[side]
         mixed = jnp.where(paired[side], (own + other) * 0.5, own)
         out_ref[:, span(c)] = jnp.where(own_valid[side] > 0.5, mixed - shift, 0.0)
-        put(c).start()
 
     @pl.when(me != 0)
     def _():
@@ -411,11 +395,6 @@
         @pl.when(lax.rem(me + d, devices) < owners)
         def _():
             scatter(d).wait_send()
-
-    @pl.loop(0, count)
-    def _(c):
-        put(c).wait()
-
 
 def per_device(n_region, n_tile, quantized, block_scales, band_width, valid_count, prior_basis):
     tokens, feats = quantized.shape
@@ -434,13 +413,10 @@
             jax.ShapeDtypeStruct((k, tokens), F32),
             jax.ShapeDtypeStruct((k, feats), F32),
         ),
-        in_specs=[smem, smem] + [pl.BlockSpec(memory_space=pltpu.HBM)] * 3,
-        out_specs=(pl.BlockSpec(memory_space=pl.ANY), vmem),
+        in_specs=[smem, smem, pl.BlockSpec(memory_space=pltpu.HBM), vmem, vmem],
+        out_specs=(vmem, vmem),
         scratch_shapes=[
-            pltpu.VMEM((k, tokens), F32),
             pltpu.VMEM((tokens, feats), BF16),
-            pltpu.VMEM(block_scales.shape, F32),
-            pltpu.VMEM((k, feats), F32),
             pltpu.VMEM((2 * k + 16, feats), F32),
             pltpu.VMEM((2 * k, feats), BF16),
             pltpu.VMEM((2, k, BAND), F32),
@@ -454,13 +430,13 @@
             pltpu.VMEM((others, feats // 128, 256), F32),
             pltpu.VMEM((k, feats), F32),
             pltpu.VMEM((feats // 128, 256), F32),
-            dma((tokens // BAND,)), dma((2,)), dma((tokens // BAND,)),
+            dma((tokens // BAND,)),
             dma((2,)), dma((2,)), dma((2,)), dma((2,)),
             dma((others,)), dma((others,)), dma(()), dma((others,)),
             dma((others,)), dma((others,)), dma((others,)), dma(()),
         ],
         compiler_params=pltpu.CompilerParams(
-            collective_id=0, has_side_effects=True, vmem_limit_bytes=67043328
+            collective_id=0, has_side_effects=True, vmem_limit_bytes=48 * 1024 * 1024
         ),
     )(band_width, valid_count, quantized, block_scales, prior_basis.T)
     return projected, basis.T

time: 49.5 us -> 48.6 us (0.982)
  Pallas kernels: 44.1 us -> 43 us
    pallas_call x1, Pallas kernels: 44.1 us -> 43 us  [per_device(): pl.pallas_call(functools.partial(kernel, n_region, n_tile, owners, width)...]
    unnamed x2 -> x8, local copies, waits for them, and re-layouts: 3.94 us -> 4.18 us
where the time goes in v4:
time: 48.6 us; the launch traced here: 48.4 us
  Pallas kernels  43 us (88%)
  local copies, waits for them, and re-layouts  4.18 us (9%)
  between operations  1.3 us (3%)
    pallas_call x1, Pallas kernels, per_device(): pl.pallas_call(functools.partial(kernel, n_region, n_tile, owners, width)...  43 us
    unnamed x8, local copies, waits for them, and re-layouts  4.18 us

profile of v4, /device:TPU:0, one launch (start us, length us, event | category | flops | bytes accessed | tf_op | source)
XLA Modules:
  0.0 48.4 jit_solution(11802615380029771941)
XLA Ops:
  1.3 0.0 copy-start
  1.3 0.9 %copy-done = f32[1024,64]{0,1:T(8,128)S(1)} copy-done((f32[1024,64]{0,1:T(8,128)S(1)}, f32[1024,64]{0,1:T(8,128)}, u32[]{:S(2)}) %copy-start) | copy-done | bytes 262168
  2.2 0.0 copy-start.1
  2.2 0.9 %copy-done.1 = f32[8,4096]{1,0:T(8,128)S(1)} copy-done((f32[8,4096]{1,0:T(8,128)S(1)}, f32[8,4096]{1,0:T(8,128)}, u32[]{:S(2)}) %copy-start.1) | copy-done | bytes 131096
  3.1 0.0 copy-start.2
  3.1 0.7 %copy-done.2 = s32[32]{0:T(128)S(1)} copy-done((s32[32]{0:T(128)S(1)}, s32[32]{0:T(128)}, u32[]{:S(2)}) %copy-start.2) | copy-done | bytes 152
  3.8 43.0 %shard_map.68 = (f32[64,4096]{1,0:T(8,128)S(1)}, f32[64,1024]{1,0:T(8,128)S(1)}) custom-call(s32[32]{0:T(128)S(1)} %copy-done.2, s32[1]{0:T(128)S(6)} %copy.9.vc_ref, bf16[4096,1024]{1,0:T(8,128)(2,1)} %q_ref.1, f32[8,4096]{1,0:T(8,128)S(1)} %copy-done.1, f32[64,1024]{1,0:T(8,128)S(1)} %bitcast.2), custom_call_target="tpu_custom_call" | custom-call | tf_op jit(solution)/shard_map/pallas_call | solution.py:410
  46.8 1.0 %copy.10 = f32[64,4096]{1,0:T(8,128)} copy(f32[64,4096]{1,0:T(8,128)S(1)} %get-tuple-element.8) | data formatting | bytes 2097152
  47.7 0.7 %copy.11 = f32[1024,64]{0,1:T(8,128)} copy(f32[1024,64]{0,1:T(8,128)S(1)} %bitcast.3) | data formatting | bytes 524288
Async XLA Ops:
  1.3 1.0 %copy-start = (f32[1024,64]{0,1:T(8,128)S(1)}, f32[1024,64]{0,1:T(8,128)}, u32[]{:S(2)}) copy-start(f32[1024,64]{0,1:T(8,128)} %param.9) | copy-start | bytes 786436
  2.2 0.9 %copy-start.1 = (f32[8,4096]{1,0:T(8,128)S(1)}, f32[8,4096]{1,0:T(8,128)}, u32[]{:S(2)}) copy-start(f32[8,4096]{1,0:T(8,128)} %sc_ref.1) | copy-start | bytes 393220
  3.1 0.7 %copy-start.2 = (s32[32]{0:T(128)S(1)}, s32[32]{0:T(128)}, u32[]{:S(2)}) copy-start(s32[32]{0:T(128)} %bw_ref.1) | copy-start | bytes 388
